TPU v7x, 256 devices: a whole 4x4x8 slice. The times are simulated.
256 devices in a mesh: row: 16 (over z_hi, x), col: 16 (over z_lo, y, core).
Axes of the slice: x: 4, y: 4, z: 8 (z_hi: 4, z_lo: 2; z = z_hi * 2 + z_lo), core: 2. Of those that a mesh axis runs over, the one named last changes fastest.
Arguments:
- visible_data: bfloat16 [512, 32768], P('col', 'row'), may hold values from 0 to 1
- hidden_uniform: float32 [512, 16384], P('row', 'col'), may hold values from 0.01 to 0.99
- visible_uniform: float32 [512, 32768], P('col', 'row'), may hold values from 0.01 to 0.99
- weights: bfloat16 [32768, 16384], P('row', 'col'), may hold values from -0.03125 to 0.03125
- visible_bias: float32 [32768], P('row'), may hold values from -4 to 4
- hidden_bias: float32 [16384], P('col'), may hold values from -4 to 4
Outputs:
- grad_weights: bfloat16 [32768, 16384], P('row', 'col')
- grad_visible: float32 [32768], P('row')
- grad_hidden: float32 [16384], P('col')
- hidden_sample: bfloat16 [512, 16384], P('row', 'col')
- reconstruction: bfloat16 [512, 32768], P('col', 'row')
All inputs are finite; a program needn't handle non-finite values.
Results may differ from a plain program's by a relative error of at most 0.0034.
Values may be sent and summed in bfloat16 or wider, within the bound.
No kernel may reach another device: no remote copies, remote signals or barrier semaphores. Data moves between devices by JAX's collectives and lax.ppermute only.
A program may use at most 64 MiB of HBM per device.

v0:
```python
import jax
import jax.numpy as jnp
from jax import lax
from jax.sharding import PartitionSpec as P


def from_everyone(array, axis):
    devices = lax.axis_size(axis)
    return lax.all_to_all(
        jnp.broadcast_to(array[None], (devices, *array.shape)), axis, 0, 0, tiled=True
    )


def laid_out(pieces, dim):
    shape = list(pieces.shape[1:])
    shape[dim] *= pieces.shape[0]
    return jnp.moveaxis(pieces, 0, dim).reshape(shape)


def collect(array, axis, dim):
    pieces = from_everyone(array, axis)
    return laid_out(pieces, dim)


def split_up(array, dim, devices):
    before, after = (array.shape[:dim], array.shape[dim + 1 :])
    return jnp.moveaxis(array.reshape(*before, devices, -1, *after), dim, 0)


def sum_at_owner(array, axis, dim):
    devices = lax.axis_size(axis)
    pieces = lax.all_to_all(split_up(array, dim, devices), axis, 0, 0, tiled=True)
    return jnp.sum(pieces, axis=0)


def side_by_side(arrays, axis, dim, along):
    ends, at = ([], 0)
    for a in arrays[:-1]:
        at += a.shape[along]
        ends.append(at)
    both = jnp.concatenate(arrays, axis=along)
    return tuple(jnp.split(lax.all_gather(both, axis, axis=dim, tiled=True), ends, axis=along))


def summed_on_arrival(array, axis, dim):
    pieces = split_up(array, dim, lax.axis_size(axis))
    arrived = lax.all_to_all(pieces, axis, split_axis=0, concat_axis=0, tiled=True)
    return arrived.astype(jnp.float32).sum(axis=0)


def relaxed(field, uniform):
    return jax.nn.sigmoid(2.0 * (field + jnp.log(uniform) - jnp.log1p(-uniform)))


def on_device(visible_data, hidden_uniform, visible_uniform, weights, visible_bias, hidden_bias):
    row_count = lax.axis_size("row")
    col_count = lax.axis_size("col")
    batch_total = visible_data.shape[0] * col_count
    hidden_rows_dev = batch_total // row_count
    visible_rows_dev = batch_total // col_count
    transposed = (((1,), (1,)), ((), ()))
    visible_full = collect(visible_data, "col", 0)

    def hidden_field(source):
        return (
            sum_at_owner(jnp.dot(source, weights, preferred_element_type=jnp.float32), "row", 0)
            + hidden_bias
        )

    field_pos = hidden_field(visible_full)
    probs_pos = jax.nn.sigmoid(field_pos).astype(jnp.bfloat16)
    sample_pos = relaxed(field_pos, hidden_uniform).astype(jnp.bfloat16)
    sample_full, probs_full = side_by_side((sample_pos, probs_pos), "row", 0, 1)
    field_neg = (
        summed_on_arrival(
            lax.dot_general(
                sample_full, weights, transposed, preferred_element_type=jnp.float32
            ).astype(jnp.bfloat16),
            "col",
            0,
        )
        + visible_bias
    )
    recon_own = relaxed(field_neg, visible_uniform).astype(jnp.bfloat16)
    recon_full = lax.all_gather(recon_own, "col", axis=0, tiled=True)
    probs_back = jax.nn.sigmoid(hidden_field(recon_full)).astype(jnp.bfloat16)
    negative_full = collect(probs_back, "row", 0)
    contract_batch = (((0,), (0,)), ((), ()))
    left_side = jnp.concatenate([visible_full, recon_full], axis=0)
    right_side = jnp.concatenate([probs_full, -negative_full], axis=0)
    difference = lax.dot_general(
        left_side, right_side, contract_batch, preferred_element_type=jnp.float32
    )
    grad_weights = (difference / batch_total).astype(jnp.bfloat16)
    grad_visible = jnp.mean(
        visible_full.astype(jnp.float32) - recon_full.astype(jnp.float32), axis=0
    )
    grad_hidden = jnp.mean(
        probs_full.astype(jnp.float32) - negative_full.astype(jnp.float32), axis=0
    )
    hidden_sample = lax.dynamic_slice_in_dim(
        sample_full, lax.axis_index("row") * hidden_rows_dev, hidden_rows_dev, 0
    )
    reconstruction = lax.dynamic_slice_in_dim(
        recon_full, lax.axis_index("col") * visible_rows_dev, visible_rows_dev, 0
    )
    return (grad_weights, grad_visible, grad_hidden, hidden_sample, reconstruction)


def solution(mesh):
    placed = (
        P("col", "row"),
        P("row", "col"),
        P("col", "row"),
        P("row", "col"),
        P("row"),
        P("col"),
    )
    return jax.shard_map(
        on_device,
        mesh=mesh,
        in_specs=placed,
        out_specs=(P("row", "col"), P("row"), P("col"), P("row", "col"), P("col", "row")),
        check_vma=False,
    )
```

profile of v0, /device:TPU:1, one launch (start us, length us, event | category | flops | bytes accessed | tf_op | source)
XLA Modules:
  0.0 346.3 jit_solution(4856000689121284117)
XLA Ops:
  7.2 1.1 broadcast_in_dim.4
  8.4 34.1 %all_to_all.25 = bf16[16,32,2048]{2,1,0:T(8,128)(2,1)S(1)} all-to-all(bf16[16,32,2048]{2,1,0:T(8,128)(2,1)S(1)} %broadcast_in_dim.4), channel_id=1, replica_groups=mesh['row'=16,'col'=16] {'col'}, dimensions={0} | all-to-all | bytes 4194304 | tf_op jit(solution)/shard_map/all_to_all | solution.py:9
  42.4 2.4 fusion.3
  44.8 58.6 %all_to_all.26 = f32[16,32,1024]{2,1,0:T(8,128)} all-to-all(f32[16,32,1024]{2,1,0:T(8,128)S(1)} %fusion.3), channel_id=1, replica_groups=mesh['row'=16,'col'=16] {'row'}, dimensions={0} | all-to-all | bytes 4194304 | tf_op jit(solution)/shard_map/all_to_all | solution.py:32
  103.5 1.7 reduce_sum.45
  105.4 0.7 pad_maximum_fusion
  106.1 57.7 %all-gather.3.cloned.1.call-done = bf16[512,2048]{1,0:T(8,128)(2,1)} async-done(((bf16[32,2048]{1,0:T(8,128)(2,1)}), bf16[512,2048]{1,0:T(8,128)(2,1)}) %all-gather.3.cloned.1.call-update) | async-done | bytes 2097168 | tf_op jit(solution)/shard_map/all_gather | solution.py:42
  163.8 4.9 %convolution_convert_fusion = bf16[512,2048]{1,0:T(8,128)(2,1)S(1)} fusion(bf16[2048,1024]{1,0:T(8,128)(2,1)} %param.9, bf16[512,2048]{1,0:T(8,128)(2,1)} %all-gather.3.cloned.1.call-done), kind=kOutput, calls=%fused_computation.8 | convolution fusion | flops 2148532224 | bytes 7340032 | tf_op jit(solution)/shard_map/dot_general | solution.py:76
  168.7 31.5 %all_to_all.27 = bf16[16,32,2048]{2,1,0:T(8,128)(2,1)S(1)} all-to-all(bf16[16,32,2048]{2,1,0:T(8,128)(2,1)S(1)} %bitcast.16), channel_id=1, replica_groups=mesh['row'=16,'col'=16] {'col'}, dimensions={0} | all-to-all | bytes 4194304 | tf_op jit(solution)/shard_map/all_to_all | solution.py:47
  201.1 0.8 divide_convert_fusion
  202.0 33.8 %all-gather.5.cloned.1.call-done = bf16[512,2048]{1,0:T(8,128)(2,1)} async-done(((bf16[32,2048]{1,0:T(8,128)(2,1)}), bf16[512,2048]{1,0:T(8,128)(2,1)}) %all-gather.5.cloned.1.call-update) | async-done | bytes 2097168 | tf_op jit(solution)/shard_map/all_gather | solution.py:85
  235.8 5.1 %fusion.12 = f32[512,1024]{1,0:T(8,128)S(1)} fusion(bf16[512,2048]{1,0:T(8,128)(2,1)} %all-gather.5.cloned.1.call-done, bf16[2048,1024]{1,0:T(8,128)(2,1)} %param.9), kind=kOutput, calls=%fused_computation.26 | convolution fusion | flops 2147483648 | bytes 8388608 | tf_op jit(solution)/shard_map/dot_general | solution.py:66
  240.9 59.4 %all_to_all.28 = f32[16,32,1024]{2,1,0:T(8,128)} all-to-all(f32[16,32,1024]{2,1,0:T(8,128)S(1)} %bitcast.17), channel_id=1, replica_groups=mesh['row'=16,'col'=16] {'row'}, dimensions={0} | all-to-all | bytes 4194304 | tf_op jit(solution)/shard_map/all_to_all | solution.py:32
  300.3 1.7 reduce_sum.47
  302.1 1.1 broadcast_in_dim.5
  303.2 5.2 %all-to-all-start.4 = ((bf16[16,32,1024]{2,1,0:T(8,128)(2,1)}), bf16[16,32,1024]{2,1,0:T(8,128)(2,1)S(1)}, u32[]{:S(2)}, u32[]{:S(2)}) async-start(bf16[16,32,1024]{2,1,0:T(8,128)(2,1)} %broadcast_in_dim.5), calls=%async_computation.4 | async-start | bytes 2097152 | tf_op jit(solution)/shard_map/all_to_all | solution.py:9
  308.3 2.8 fusion.11
  311.2 0.6 constant_dynamic-slice_fusion.1
  311.8 0.8 subtract_reduce_fusion
  312.6 0.6 broadcast_multiply_fusion
  313.2 0.7 constant_dynamic-slice_fusion
  313.9 16.7 %all-to-all-done.4 = bf16[16,32,1024]{2,1,0:T(8,128)(2,1)S(1)} async-done(((bf16[16,32,1024]{2,1,0:T(8,128)(2,1)}), bf16[16,32,1024]{2,1,0:T(8,128)(2,1)S(1)}, u32[]{:S(2)}, u32[]{:S(2)}) %all-to-all-start.4) | async-done | bytes 1048608 | tf_op jit(solution)/shard_map/all_to_all | solution.py:9
  330.6 1.8 fusion.8
  333.2 6.2 %multiply_convert_fusion = bf16[2048,1024]{1,0:T(8,128)(2,1)} fusion(bf16[512,2048]{1,0:T(8,128)(2,1)S(1)} %copy-done.1, bf16[512,2048]{1,0:T(8,128)(2,1)S(1)} %bitcast.15, bf16[512,1024]{1,0:T(8,128)(2,1)S(1)} %bitcast.18, bf16[512,1024]{1,0:T(8,128)(2,1)S(1)} %copy-done.2), kind=kOutput, calls=%fused_computation | convolution fusion | flops 4311744512 | bytes 10485760 | tf_op jit(solution)/shard_map/dot_general | solution.py:91
  (25 shorter events, 2.1 us)
Async XLA Ops:
  7.2 156.7 %all-gather.3.cloned.1.call-start = ((), (), s32[]{:S(2)}) async-start(), calls=%async_computation.5 | async-start | bytes 2228224 | tf_op jit(solution)/shard_map/all_gather | solution.py:42
  8.4 34.1 %copy-start.7 = (bf16[2048,1024]{1,0:T(8,128)(2,1)S(1)}, bf16[2048,1024]{1,0:T(8,128)(2,1)}, u32[]{:S(2)}) copy-start(bf16[2048,1024]{1,0:T(8,128)(2,1)} %param.9) | copy-start | bytes 12582916
  103.4 1.8 copy-start.4
  103.4 1.8 copy-start.5
  106.0 129.7 %all-gather.5.cloned.1.call-start = ((), (), s32[]{:S(2)}) async-start(), calls=%async_computation.6 | async-start | bytes 2228224 | tf_op jit(solution)/shard_map/all_gather | solution.py:85
  200.2 1.0 copy-start.3
  200.2 1.0 copy-start.6
  303.2 27.4 %all-to-all-start.4 = ((bf16[16,32,1024]{2,1,0:T(8,128)(2,1)}), bf16[16,32,1024]{2,1,0:T(8,128)(2,1)S(1)}, u32[]{:S(2)}, u32[]{:S(2)}) async-start(bf16[16,32,1024]{2,1,0:T(8,128)(2,1)} %broadcast_in_dim.5), calls=%async_computation.4 | async-start | bytes 2097152 | tf_op jit(solution)/shard_map/all_to_all | solution.py:9
  308.3 3.5 %copy-start = (bf16[512,2048]{1,0:T(8,128)(2,1)S(1)}, bf16[512,2048]{1,0:T(8,128)(2,1)}, u32[]{:S(2)}) copy-start(bf16[512,2048]{1,0:T(8,128)(2,1)} %all-gather.5.cloned.1.call-done) | copy-start | bytes 6291460
  330.6 2.6 copy-start.1
  330.6 2.6 copy-start.2
Sparse Core Ops, SparseCore 0:
  106.2 57.6 all-gather.2
  202.1 33.6 all-gather.4
where the time goes:
time: 353 us; the launch traced here: 346 us
  blocking collectives  184 us (52%)
  waiting for transfers between devices  108 us (31%)
  matrix products  18.6 us (5%)
  between operations  14.2 us (4%)
  other arithmetic  9.55 us (3%)
  local copies, waits for them, and re-layouts  6.97 us (2%)
  starting transfers between devices  5.24 us (1%)
    all_to_all x2, blocking collectives, sum_at_owner(): lax.all_to_all(split_up(array, dim, devices), axis, 0, 0, tiled=True)  118 us
    all_gather x1, waiting for transfers between devices, side_by_side(): lax.all_gather(both, axis, axis=dim, tiled=True)  57.7 us
    all_to_all x1, blocking collectives, from_everyone(): lax.all_to_all(jnp.broadcast_to(array[None], (devices, *array.shape)), ax...  34.1 us
    all_gather x1, waiting for transfers between devices, on_device(): recon_full = lax.all_gather(recon_own, 'col', axis=0, tiled=True)  33.8 us
    all_to_all x1, blocking collectives, summed_on_arrival(): lax.all_to_all(pieces, axis, split_axis=0, concat_axis=0, tiled=True)  31.5 us
    all_to_all x1, waiting for transfers between devices, from_everyone(): lax.all_to_all(jnp.broadcast_to(array[None], (devices, *array.shape)), ax...  16.7 us
    dot_general x2, matrix products, hidden_field(): jnp.dot(source, weights, preferred_element_type=jnp.float32)  7.51 us
  transfers between devices with their start and end apart: 3, of which 3 were waited for; matrix products, arithmetic and copies ran while one was open for 2% of the time, Pallas kernels for 0%

commit v1 on v0

v1 whole, which is shorter than its diff:
```python
import functools

import jax
import jax.numpy as jnp
from jax import lax
from jax.experimental import pallas as pl
from jax.experimental.pallas import tpu as pltpu
from jax.sharding import PartitionSpec as P

F32, BF16 = jnp.float32, jnp.bfloat16


def flip(array, axis, bits):
    return lax.ppermute(array, axis, [(i, i ^ bits) for i in range(16)])


def spread(array, axis, step):
    return [array] + [flip(array, axis, s * step) for s in (1, 2, 3)]


def row_to_index(p):
    return (p & 3) * 4 + (p >> 2)


def col_to_index(p):
    return ((p >> 1) & 3) * 4 + (p >> 3) * 2 + (p & 1)


def put_rows(q, acc, outs, rows, to_row):
    for piece in range(4):
        for sub in range(4):
            if to_row:
                source = col_to_index((sub * 4 + piece) ^ q)
            else:
                source = row_to_index(((sub >> 1) * 8 + piece * 2 + (sub & 1)) ^ q)
            block = acc[pl.ds(pl.multiple_of(source * rows, rows), rows), :]
            out = outs[piece]
            out[sub * rows : (sub + 1) * rows, :] = block.astype(out.dtype)


def forward_kernel(steps, rows, q_ref, a0, a1, a2, a3, own, other, *rest):
    outs, (lhs, acc) = rest[:4], rest[4:]
    step = pl.program_id(0)
    n = a0.shape[0]

    @pl.when(step == 0)
    def _():
        for i, a in enumerate((a0, a1, a2, a3)):
            lhs[i * n : (i + 1) * n, :] = a[...]

    @pl.when(step < steps)
    def _():
        acc[...] = jnp.dot(lhs[...], own[...], preferred_element_type=F32)

    @pl.when(step >= steps)
    def _():
        acc[...] = jnp.dot(lhs[...], other[...], preferred_element_type=F32)

    put_rows(q_ref[0], acc, outs, rows, True)


def forward(q, pieces, own, other, tile=512):
    n, depth = pieces[0].shape
    width = own.shape[1]
    steps = width // tile
    whole = pl.BlockSpec((n, depth), lambda j, q: (0, 0))
    out = [jax.ShapeDtypeStruct((n, 2 * width), F32)] + [
        jax.ShapeDtypeStruct((n, 2 * width), BF16) for _ in range(3)
    ]
    return pl.pallas_call(
        functools.partial(forward_kernel, steps, n // 4),
        out_shape=out,
        grid_spec=pltpu.PrefetchScalarGridSpec(
            num_scalar_prefetch=1,
            grid=(2 * steps,),
            in_specs=[whole] * 4
            + [
                pl.BlockSpec((depth, tile), lambda j, q: (0, jnp.minimum(j, steps - 1))),
                pl.BlockSpec((depth, tile), lambda j, q: (0, jnp.maximum(j - steps, 0))),
            ],
            out_specs=[pl.BlockSpec((n, tile), lambda j, q: (0, j))] * 4,
            scratch_shapes=[pltpu.VMEM((4 * n, depth), BF16), pltpu.VMEM((4 * n, tile), F32)],
        ),
        compiler_params=pltpu.CompilerParams(vmem_limit_bytes=40 << 20),
        cost_estimate=pl.CostEstimate(
            flops=2 * 4 * n * depth * 2 * width,
            bytes_accessed=4 * depth * width + 10 * n * depth + 10 * n * width,
            transcendentals=0,
        ),
    )(q, *pieces, own, other)


def backward_kernel(rows, q_ref, a0, a1, a2, a3, own, other, *rest):
    outs, (lhs, acc) = rest[:4], rest[4:]
    n = a0.shape[0]

    @pl.when(pl.program_id(0) == 0)
    def _():
        for i, a in enumerate((a0, a1, a2, a3)):
            lhs[i * n : (i + 1) * n, :] = a[...]

    width = own.shape[1]
    transposed = (((1,), (1,)), ((), ()))
    acc[...] = lax.dot_general(
        lhs[:, :width], own[...], transposed, preferred_element_type=F32
    ) + lax.dot_general(lhs[:, width:], other[...], transposed, preferred_element_type=F32)
    put_rows(q_ref[0], acc, outs, rows, False)


def backward(q, pieces, own, other, tile=512):
    n, depth = pieces[0].shape
    height, width = own.shape
    whole = pl.BlockSpec((n, depth), lambda j, q: (0, 0))
    out = [jax.ShapeDtypeStruct((n, height), F32)] + [
        jax.ShapeDtypeStruct((n, height), BF16) for _ in range(3)
    ]
    return pl.pallas_call(
        functools.partial(backward_kernel, n // 4),
        out_shape=out,
        grid_spec=pltpu.PrefetchScalarGridSpec(
            num_scalar_prefetch=1,
            grid=(height // tile,),
            in_specs=[whole] * 4 + [pl.BlockSpec((tile, width), lambda j, q: (j, 0))] * 2,
            out_specs=[pl.BlockSpec((n, tile), lambda j, q: (0, j))] * 4,
            scratch_shapes=[pltpu.VMEM((4 * n, depth), BF16), pltpu.VMEM((4 * n, tile), F32)],
        ),
        compiler_params=pltpu.CompilerParams(vmem_limit_bytes=40 << 20),
        cost_estimate=pl.CostEstimate(
            flops=2 * 4 * n * depth * height,
            bytes_accessed=4 * height * width + 10 * n * depth + 10 * n * height,
            transcendentals=0,
        ),
    )(q, *pieces, own, other)


def gradient_kernel(total, rows, q_ref, *refs):
    (v, v_other, r, r_other, pos, neg) = (refs[0:4], refs[4:8], refs[8:12], refs[12:16], refs[16:20], refs[20:24])
    grad, grad_visible, grad_hidden, raw, probs, left = refs[24:]
    n = v[0].shape[0]
    half = 4 * n
    q = q_ref[0]

    @pl.when(pl.program_id(0) == 0)
    def _():
        for sign, pieces in enumerate((pos, neg)):
            for i, piece in enumerate(pieces):
                raw[i * 2 * n : (i + 1) * 2 * n, :] = piece[...]
            for other in range(2):
                for p in range(16):
                    source = row_to_index(p ^ q ^ other) * 2 + other
                    at = (sign * 2 + other) * half + col_to_index(p) * rows
                    block = raw[pl.ds(pl.multiple_of(source * rows, rows), rows), :]
                    probs[at : at + rows, :] = -block if sign else block
        grad_hidden[...] = jnp.sum(probs[...].astype(F32), axis=0, keepdims=True) / total

    for k, pieces in enumerate((v, v_other, r, r_other)):
        for i, piece in enumerate(pieces):
            left[k * half + i * n : k * half + (i + 1) * n, :] = piece[...]
    values = left[...]
    grad[...] = (
        lax.dot_general(values, probs[...], (((0,), (0,)), ((), ())), preferred_element_type=F32)
        / total
    ).astype(grad.dtype)
    grad_visible[...] = (
        jnp.sum(left[: 2 * half, :].astype(F32), axis=0, keepdims=True)
        - jnp.sum(left[2 * half :, :].astype(F32), axis=0, keepdims=True)
    ) / total


def gradient(q, total, v, v_other, r, r_other, pos, neg, tile=256):
    n, height = v[0].shape
    width = pos[0].shape[1]
    return pl.pallas_call(
        functools.partial(gradient_kernel, total, n // 4),
        out_shape=[
            jax.ShapeDtypeStruct((height, width), BF16),
            jax.ShapeDtypeStruct((1, height), F32),
            jax.ShapeDtypeStruct((1, width), F32),
        ],
        grid_spec=pltpu.PrefetchScalarGridSpec(
            num_scalar_prefetch=1,
            grid=(height // tile,),
            in_specs=[pl.BlockSpec((n, tile), lambda j, q: (0, j))] * 16
            + [pl.BlockSpec((2 * n, width), lambda j, q: (0, 0))] * 8,
            out_specs=[
                pl.BlockSpec((tile, width), lambda j, q: (j, 0)),
                pl.BlockSpec((1, tile), lambda j, q: (0, j)),
                pl.BlockSpec((1, width), lambda j, q: (0, 0)),
            ],
            scratch_shapes=[
                pltpu.VMEM((8 * n, width), BF16),
                pltpu.VMEM((16 * n, width), BF16),
                pltpu.VMEM((16 * n, tile), BF16),
            ],
        ),
        compiler_params=pltpu.CompilerParams(vmem_limit_bytes=40 << 20),
        cost_estimate=pl.CostEstimate(
            flops=2 * 16 * n * height * width,
            bytes_accessed=2 * height * width + 32 * n * height + 32 * n * width,
            transcendentals=0,
        ),
    )(q, *v, *v_other, *r, *r_other, *pos, *neg)


def on_device(visible_data, hidden_uniform, visible_uniform, weights, visible_bias, hidden_bias):
    row, col = lax.axis_index("row"), lax.axis_index("col")
    core = col & 1
    block, visibles = visible_data.shape
    hiddens = weights.shape[1]
    half = block // 2
    total = block * 16
    q = (row ^ col).astype(jnp.int32).reshape(1)

    def cut(array):
        return (
            lax.dynamic_slice_in_dim(array, core * half, half, 0),
            lax.dynamic_slice_in_dim(array, (1 - core) * half, half, 0),
        )

    def swap(array):
        return flip(array, "col", 1)

    def whole_block(mine, others):
        first = jnp.where(core == 0, mine, others)
        return jnp.concatenate([first, jnp.where(core == 0, others, mine)], axis=0)

    mine, others = cut(visible_data)
    visible = jnp.concatenate([mine, swap(others)], axis=0)
    weights_other = swap(weights)
    bias_h = jnp.concatenate([hidden_bias, swap(hidden_bias)])
    noise = jnp.log(hidden_uniform) - jnp.log1p(-hidden_uniform)
    mine, others = cut(noise)
    noise_h = jnp.concatenate([mine, swap(others)], axis=1)
    noise = jnp.log(visible_uniform) - jnp.log1p(-visible_uniform)
    mine, others = cut(noise)
    noise_v = jnp.concatenate([mine, swap(others)], axis=0)

    def gather_col(array):
        both = jnp.concatenate([array, flip(array, "col", 8)], axis=0)
        return spread(both, "col", 2)

    def gather_row(array):
        all_zh = jnp.concatenate(spread(array, "row", 4), axis=0)
        return spread(all_zh, "row", 1)

    def sum_row(pieces):
        arrived = [pieces[0]] + [flip(pieces[s], "row", s) for s in (1, 2, 3)]
        partial = sum(a.astype(F32) for a in arrived)
        n = partial.shape[0] // 4
        part = [partial[i * n : (i + 1) * n] for i in range(4)]
        return part[0] + sum(flip(part[s].astype(BF16), "row", 4 * s).astype(F32) for s in (1, 2, 3))

    def sum_col(pieces):
        arrived = [pieces[0]] + [flip(pieces[s], "col", 2 * s) for s in (1, 2, 3)]
        partial = sum(a.astype(F32) for a in arrived)
        n = partial.shape[0] // 2
        return partial[:n] + flip(partial[n:].astype(BF16), "col", 8).astype(F32)

    def share(probs):
        return gather_row(jnp.concatenate([probs[:, :hiddens], swap(probs[:, hiddens:])], axis=0))

    visible_all = gather_col(visible)
    field_pos = sum_row(forward(q, visible_all, weights, weights_other)) + bias_h
    probs_pos = jax.nn.sigmoid(field_pos).astype(BF16)
    sample = jax.nn.sigmoid(2.0 * (field_pos + noise_h)).astype(BF16)
    sample_all = gather_row(sample)
    field_neg = sum_col(backward(q, sample_all, weights, weights_other)) + visible_bias
    recon = jax.nn.sigmoid(2.0 * (field_neg + noise_v)).astype(BF16)
    recon_all = gather_col(recon)
    field_back = sum_row(forward(q, recon_all, weights, weights_other)) + bias_h
    probs_neg = jax.nn.sigmoid(field_back).astype(BF16)

    grad_weights, grad_visible, grad_hidden = gradient(
        q,
        total,
        visible_all,
        [swap(a) for a in visible_all],
        recon_all,
        [swap(a) for a in recon_all],
        share(probs_pos),
        share(probs_neg),
    )
    hidden_sample = whole_block(sample[:, :hiddens], swap(sample[:, hiddens:]))
    reconstruction = whole_block(recon[:half], swap(recon[half:]))
    return (
        grad_weights,
        grad_visible.reshape(-1),
        grad_hidden.reshape(-1),
        hidden_sample,
        reconstruction,
    )


def solution(mesh):
    placed = (
        P("col", "row"),
        P("row", "col"),
        P("col", "row"),
        P("row", "col"),
        P("row"),
        P("col"),
    )
    return jax.shard_map(
        on_device,
        mesh=mesh,
        in_specs=placed,
        out_specs=(P("row", "col"), P("row"), P("col"), P("row", "col"), P("col", "row")),
        check_vma=False,
    )
```

time: 353 us -> 246 us (0.70); the launches traced: 346 us -> 243 us
  blocking collectives: 184 us -> 0 us
  starting transfers between devices: 5.24 us -> 113 us
  Pallas kernels: 0 us -> 25.9 us
  matrix products: 18.6 us -> 0 us
  between operations: 14.2 us -> 1.18 us
  waiting for transfers between devices: 108 us -> 95.7 us
  other arithmetic: 9.55 us -> 2.2 us
    all_to_all x4 -> x0, blocking collectives: 184 us -> none  [the longest x2 118 us: sum_at_owner(): lax.all_to_all(split_up(array, dim, devices), axis, 0, 0, tiled=True)]
    ppermute x0 -> x59, starting transfers between devices: none -> 113 us  [flip(): return lax.ppermute(array, axis, [(i, i ^ bits) for i in range(16)])]
    ppermute x0 -> x59, waiting for transfers between devices: none -> 95.7 us  [flip(): return lax.ppermute(array, axis, [(i, i ^ bits) for i in range(16)])]
    all_gather x2 -> x0, waiting for transfers between devices: 91.5 us -> none  [the longest x1 57.7 us: side_by_side(): lax.all_gather(both, axis, axis=dim, tiled=True)]
    pallas_call x0 -> x4, Pallas kernels: none -> 25.9 us  [the longest x2 11.8 us: forward(): pl.pallas_call(functools.partial(forward_kernel, steps, n // 4), out_shap...]
    dot_general x4 -> x0, matrix products: 18.6 us -> none  [the longest x2 7.51 us: hidden_field(): jnp.dot(source, weights, preferred_element_type=jnp.float32)]
    all_to_all x1 -> x0, waiting for transfers between devices: 16.7 us -> none  [from_everyone(): lax.all_to_all(jnp.broadcast_to(array[None], (devices, *array.shape)), ax...]
    reduce_sum x5 -> x0, other arithmetic: 6.46 us -> none  [the longest x2 3.46 us: sum_at_owner(): return jnp.sum(pieces, axis=0)]
  transfers between devices with their start and end apart: 3 -> 59, of which waited for: 3 -> 26; matrix products, arithmetic and copies ran while one was open for 2% -> 1% of each run, Pallas kernels for 0% -> 5%
where the time goes in v1:
time: 246 us; the launch traced here: 243 us
  starting transfers between devices  113 us (46%)
  waiting for transfers between devices  95.7 us (39%)
  Pallas kernels  25.9 us (11%)
  local copies, waits for them, and re-layouts  5.44 us (2%)
    ppermute x59, starting transfers between devices, flip(): return lax.ppermute(array, axis, [(i, i ^ bits) for i in range(16)])  113 us
    ppermute x59, waiting for transfers between devices, flip(): return lax.ppermute(array, axis, [(i, i ^ bits) for i in range(16)])  95.7 us
    pallas_call x2, Pallas kernels, forward(): pl.pallas_call(functools.partial(forward_kernel, steps, n // 4), out_shap...  11.8 us
    pallas_call x1, Pallas kernels, gradient(): pl.pallas_call(functools.partial(gradient_kernel, total, n // 4), out_sha...  9.01 us
    pallas_call x1, Pallas kernels, backward(): pl.pallas_call(functools.partial(backward_kernel, n // 4), out_shape=out,...  5.06 us
  transfers between devices with their start and end apart: 59, of which 26 were waited for; matrix products, arithmetic and copies ran while one was open for 1% of the time, Pallas kernels for 5%

profile of v1, /device:TPU:1, one launch (start us, length us, event | category | flops | bytes accessed | tf_op | source)
XLA Modules:
  0.0 242.9 jit_solution(2964986300812305354)
XLA Ops:
  5.0 5.9 %collective-permute-done = bf16[16,2048]{1,0:T(8,128)(2,1)S(1)} collective-permute-done((bf16[16,2048]{1,0:T(8,128)(2,1)S(1)}, bf16[16,2048]{1,0:T(8,128)(2,1)S(1)}, u32[]{:S(2)}, u32[]{:S(2)}) %collective-permute-start) | collective-permute-done | bytes 65568 | tf_op jit(solution)/shard_map/ppermute | solution.py:14
  11.0 4.7 %collective-permute-done.1 = bf16[32,2048]{1,0:T(8,128)(2,1)S(1)} collective-permute-done((bf16[32,2048]{1,0:T(8,128)(2,1)S(1)}, bf16[32,2048]{1,0:T(8,128)(2,1)S(1)}, u32[]{:S(2)}, u32[]{:S(2)}) %collective-permute-start.1) | collective-permute-done | bytes 131104 | tf_op jit(solution)/shard_map/ppermute | solution.py:14
  21.1 8.1 %collective-permute-done.4.a3.refs_3_ = bf16[64,2048]{1,0:T(8,128)(2,1)S(1)} collective-permute-done((bf16[64,2048]{1,0:T(8,128)(2,1)S(1)}, bf16[64,2048]{1,0:T(8,128)(2,1)S(1)}, u32[]{:S(2)}, u32[]{:S(2)}) %collective-permute-start.4) | collective-permute-done | bytes 262176 | tf_op jit(solution)/shard_map/ppermute | solution.py:14
  31.8 6.0 %shard_map.101 = (f32[64,2048]{1,0:T(8,128)S(1)}, bf16[64,2048]{1,0:T(8,128)(2,1)S(1)}, bf16[64,2048]{1,0:T(8,128)(2,1)S(1)}, bf16[64,2048]{1,0:T(8,128)(2,1)S(1)}) custom-call(s32[1]{0:T(128)} %bitcast.q_ref, bf16[64,2048]{1,0:T(8,128)(2,1)S(1)} %pad_maximum_fusion.a0.refs_0_, bf16[64,2048]{1,0:T(8,128)(2,1)S(1)} %collective-permute-done.2.a1.refs_1_, ...), custom_call_target="tpu_custom_call" | custom-call | flops 2147483648 | bytes 10354688 | tf_op jit(solution)/shard_map/pallas_call | solution.py:70
  45.1 5.5 %collective-permute-done.11 = bf16[64,2048]{1,0:T(8,128)(2,1)S(1)} collective-permute-done((bf16[64,2048]{1,0:T(8,128)(2,1)S(1)}, bf16[64,2048]{1,0:T(8,128)(2,1)S(1)}, u32[]{:S(2)}, u32[]{:S(2)}) %collective-permute-start.11) | collective-permute-done | bytes 262176 | tf_op jit(solution)/shard_map/ppermute | solution.py:14
  50.6 3.4 %collective-permute-done.12 = bf16[64,2048]{1,0:T(8,128)(2,1)S(1)} collective-permute-done((bf16[64,2048]{1,0:T(8,128)(2,1)S(1)}, bf16[64,2048]{1,0:T(8,128)(2,1)S(1)}, u32[]{:S(2)}, u32[]{:S(2)}) %collective-permute-start.12) | collective-permute-done | bytes 262176 | tf_op jit(solution)/shard_map/ppermute | solution.py:14
  57.3 3.6 %collective-permute-start.15 = (bf16[16,2048]{1,0:T(8,128)(2,1)S(1)}, bf16[16,2048]{1,0:T(8,128)(2,1)S(1)}, u32[]{:S(2)}, u32[]{:S(2)}) collective-permute-start(bf16[16,2048]{1,0:T(8,128)(2,1)S(1)} %get-tuple-element.45), channel_id=1, source_target_pairs={{0,192},{16,208},{32,224},{48,240},{64,128},{80,144},{96,160},{112... | collective-permute-start | bytes 196616 | tf_op jit(solution)/shard_map/ppermute | solution.py:14
  63.1 5.5 %collective-permute-done.14 = bf16[16,2048]{1,0:T(8,128)(2,1)S(1)} collective-permute-done((bf16[16,2048]{1,0:T(8,128)(2,1)S(1)}, bf16[16,2048]{1,0:T(8,128)(2,1)S(1)}, u32[]{:S(2)}, u32[]{:S(2)}) %collective-permute-start.14) | collective-permute-done | bytes 65568 | tf_op jit(solution)/shard_map/ppermute | solution.py:14
  68.8 3.9 %collective-permute-start.19 = (bf16[16,2048]{1,0:T(8,128)(2,1)S(1)}, bf16[16,2048]{1,0:T(8,128)(2,1)S(1)}, u32[]{:S(2)}, u32[]{:S(2)}) collective-permute-start(bf16[16,2048]{1,0:T(8,128)(2,1)S(1)} %get-tuple-element.40), channel_id=1, source_target_pairs={{0,128},{16,144},{32,160},{48,176},{64,192},{80,208},{96,224},{112... | collective-permute-start | bytes 196616 | tf_op jit(solution)/shard_map/ppermute | solution.py:14
  81.9 6.1 %collective-permute-done.23.a3 = bf16[64,2048]{1,0:T(8,128)(2,1)S(1)} collective-permute-done((bf16[64,2048]{1,0:T(8,128)(2,1)S(1)}, bf16[64,2048]{1,0:T(8,128)(2,1)S(1)}, u32[]{:S(2)}, u32[]{:S(2)}) %collective-permute-start.23) | collective-permute-done | bytes 262176 | tf_op jit(solution)/shard_map/ppermute | solution.py:14
  88.5 5.1 %shard_map.102 = (f32[64,2048]{1,0:T(8,128)S(1)}, bf16[64,2048]{1,0:T(8,128)(2,1)S(1)}, bf16[64,2048]{1,0:T(8,128)(2,1)S(1)}, bf16[64,2048]{1,0:T(8,128)(2,1)S(1)}) custom-call(s32[1]{0:T(128)} %bitcast.q_ref, bf16[64,2048]{1,0:T(8,128)(2,1)S(1)} %pad_maximum_fusion.1.a0, bf16[64,2048]{1,0:T(8,128)(2,1)S(1)} %collective-permute-done.21.a1, ...), custom_call_target="tpu_custom_call" | custom-call | flops 2147483648 | bytes 11010048 | tf_op jit(solution)/shard_map/pallas_call | solution.py:117
  98.2 6.8 %collective-permute-start.28 = (f32[16,2048]{1,0:T(8,128)S(1)}, f32[16,2048]{1,0:T(8,128)S(1)}, u32[]{:S(2)}, u32[]{:S(2)}) collective-permute-start(f32[16,2048]{1,0:T(8,128)S(1)} %get-tuple-element.48), channel_id=1, source_target_pairs={{0,1},{1,0},{2,3},{3,2},{4,5},{5,4},{6,7},{7,6},{8,9},{9,8},{10,11... | collective-permute-start | bytes 393224 | tf_op jit(solution)/shard_map/ppermute | solution.py:14
  107.6 4.1 %collective-permute-done.27 = bf16[32,2048]{1,0:T(8,128)(2,1)S(1)} collective-permute-done((bf16[32,2048]{1,0:T(8,128)(2,1)S(1)}, bf16[32,2048]{1,0:T(8,128)(2,1)S(1)}, u32[]{:S(2)}, u32[]{:S(2)}) %collective-permute-start.27) | collective-permute-done | bytes 131104 | tf_op jit(solution)/shard_map/ppermute | solution.py:14
  111.9 3.8 %collective-permute-done.29 = bf16[32,2048]{1,0:T(8,128)(2,1)S(1)} collective-permute-done((bf16[32,2048]{1,0:T(8,128)(2,1)S(1)}, bf16[32,2048]{1,0:T(8,128)(2,1)S(1)}, u32[]{:S(2)}, u32[]{:S(2)}) %collective-permute-start.29) | collective-permute-done | bytes 131104 | tf_op jit(solution)/shard_map/ppermute | solution.py:14
  119.1 10.4 %collective-permute-start.37 = (bf16[16,1024]{1,0:T(8,128)(2,1)S(1)}, bf16[16,1024]{1,0:T(8,128)(2,1)S(1)}, u32[]{:S(2)}, u32[]{:S(2)}) collective-permute-start(bf16[16,1024]{1,0:T(8,128)(2,1)S(1)} %get-tuple-element.62), channel_id=1, source_target_pairs={{0,1},{1,0},{2,3},{3,2},{4,5},{5,4},{6,7},{7,6},{8,9},{9,8},{10,11... | collective-permute-start | bytes 98312 | tf_op jit(solution)/shard_map/ppermute | solution.py:14
  133.6 5.8 %shard_map.103 = (f32[64,2048]{1,0:T(8,128)S(1)}, bf16[64,2048]{1,0:T(8,128)(2,1)S(1)}, bf16[64,2048]{1,0:T(8,128)(2,1)S(1)}, bf16[64,2048]{1,0:T(8,128)(2,1)S(1)}) custom-call(s32[1]{0:T(128)} %bitcast.q_ref, bf16[64,2048]{1,0:T(8,128)(2,1)S(1)} %pad_maximum_fusion.2.a0.refs_8_, bf16[64,2048]{1,0:T(8,128)(2,1)S(1)} %collective-permute-done.30.a1.refs_9_, ...), custom_call_target="tpu_custom_call" | custom-call | flops 2147483648 | bytes 10354688 | tf_op jit(solution)/shard_map/pallas_call | solution.py:70
  143.5 6.1 %collective-permute-start.8 = (bf16[64,2048]{1,0:T(8,128)(2,1)S(1)}, bf16[64,2048]{1,0:T(8,128)(2,1)S(1)}, u32[]{:S(2)}, u32[]{:S(2)}) collective-permute-start(bf16[64,2048]{1,0:T(8,128)(2,1)S(1)} %collective-permute-done.4.a3.refs_3_), channel_id=1, source_target_pairs={{0,1},{1,0},{2,3},{3,2},{4,5},{5,4},{6,7},{7,6},{8,9},{9,8},{10,11... | collective-permute-start | bytes 786440 | tf_op jit(solution)/shard_map/ppermute | solution.py:14
  149.6 12.4 %collective-permute-start.39 = (bf16[32,1024]{1,0:T(8,128)(2,1)S(1)}, bf16[32,1024]{1,0:T(8,128)(2,1)S(1)}, u32[]{:S(2)}, u32[]{:S(2)}) collective-permute-start(bf16[32,1024]{1,0:T(8,128)(2,1)S(1)} %pad_maximum_fusion.5), channel_id=1, source_target_pairs={{0,128},{16,144},{32,160},{48,176},{64,192},{80,208},{96,224},{112... | collective-permute-start | bytes 196616 | tf_op jit(solution)/shard_map/ppermute | solution.py:14
  179.3 6.7 %collective-permute-start.50 = (bf16[16,1024]{1,0:T(8,128)(2,1)S(1)}, bf16[16,1024]{1,0:T(8,128)(2,1)S(1)}, u32[]{:S(2)}, u32[]{:S(2)}) collective-permute-start(bf16[16,1024]{1,0:T(8,128)(2,1)S(1)} %get-tuple-element.59), channel_id=1, source_target_pairs={{0,1},{1,0},{2,3},{3,2},{4,5},{5,4},{6,7},{7,6},{8,9},{9,8},{10,11... | collective-permute-start | bytes 98312 | tf_op jit(solution)/shard_map/ppermute | solution.py:14
  192.2 9.0 %collective-permute-done.43.refs_19_ = bf16[128,1024]{1,0:T(8,128)(2,1)S(1)} collective-permute-done((bf16[128,1024]{1,0:T(8,128)(2,1)S(1)}, bf16[128,1024]{1,0:T(8,128)(2,1)S(1)}, u32[]{:S(2)}, u32[]{:S(2)}) %collective-permute-start.43) | collective-permute-done | bytes 262176 | tf_op jit(solution)/shard_map/ppermute | solution.py:14
  203.7 7.6 %collective-permute-done.52 = bf16[32,1024]{1,0:T(8,128)(2,1)S(1)} collective-permute-done((bf16[32,1024]{1,0:T(8,128)(2,1)S(1)}, bf16[32,1024]{1,0:T(8,128)(2,1)S(1)}, u32[]{:S(2)}, u32[]{:S(2)}) %collective-permute-start.52) | collective-permute-done | bytes 65568 | tf_op jit(solution)/shard_map/ppermute | solution.py:14
  211.2 5.2 %collective-permute-done.53 = bf16[32,1024]{1,0:T(8,128)(2,1)S(1)} collective-permute-done((bf16[32,1024]{1,0:T(8,128)(2,1)S(1)}, bf16[32,1024]{1,0:T(8,128)(2,1)S(1)}, u32[]{:S(2)}, u32[]{:S(2)}) %collective-permute-start.53) | collective-permute-done | bytes 65568 | tf_op jit(solution)/shard_map/ppermute | solution.py:14
  222.9 10.8 %collective-permute-done.56.refs_23_ = bf16[128,1024]{1,0:T(8,128)(2,1)S(1)} collective-permute-done((bf16[128,1024]{1,0:T(8,128)(2,1)S(1)}, bf16[128,1024]{1,0:T(8,128)(2,1)S(1)}, u32[]{:S(2)}, u32[]{:S(2)}) %collective-permute-start.56) | collective-permute-done | bytes 262176 | tf_op jit(solution)/shard_map/ppermute | solution.py:14
  233.7 9.0 %shard_map.104 = (bf16[2048,1024]{1,0:T(8,128)(2,1)}, f32[1,2048]{1,0:T(1,128)}, f32[1,1024]{1,0:T(1,128)}) custom-call(s32[1]{0:T(128)} %bitcast.q_ref, bf16[64,2048]{1,0:T(8,128)(2,1)S(1)} %pad_maximum_fusion.a0.refs_0_, bf16[64,2048]{1,0:T(8,128)(2,1)S(1)} %collective-permute-done.2.a1.refs_1_, bf16[64,2048]{1,0:T(8,128)(2,1)S(1)} %collective-permute-done.3.a2.refs_2_, ...), custom_call_target="tpu_custom_call" | custom-call | flops 4294967296 | bytes 10485760 | tf_op jit(solution)/shard_map/pallas_call | solution.py:173
  (149 shorter events, 86.1 us)
Async XLA Ops:
  0.6 28.9 %collective-permute-start.9 = (bf16[2048,1024]{1,0:T(8,128)(2,1)}, bf16[2048,1024]{1,0:T(8,128)(2,1)}, u32[]{:S(2)}, u32[]{:S(2)}) collective-permute-start(bf16[2048,1024]{1,0:T(8,128)(2,1)} %own.5), channel_id=1, source_target_pairs={{0,1},{1,0},{2,3},{3,2},{4,5},{5,4},{6,7},{7,6},{8,9},{9,8},{10,11... | collective-permute-start | bytes 12582920 | tf_op jit(solution)/shard_map/ppermute | solution.py:14
  15.7 13.5 %collective-permute-start.4 = (bf16[64,2048]{1,0:T(8,128)(2,1)S(1)}, bf16[64,2048]{1,0:T(8,128)(2,1)S(1)}, u32[]{:S(2)}, u32[]{:S(2)}) collective-permute-start(bf16[64,2048]{1,0:T(8,128)(2,1)S(1)} %pad_maximum_fusion.a0.refs_0_), channel_id=1, source_target_pairs={{0,6},{1,7},{2,4},{3,5},{4,2},{5,3},{6,0},{7,1},{8,14},{9,15},{10,... | collective-permute-start | bytes 786440 | tf_op jit(solution)/shard_map/ppermute | solution.py:14
  19.0 42.8 %collective-permute-start.16 = (f32[1024]{0:T(1024)}, f32[1024]{0:T(1024)S(1)}, u32[]{:S(2)}, u32[]{:S(2)}) collective-permute-start(f32[1024]{0:T(1024)} %param.11), channel_id=1, source_target_pairs={{0,1},{1,0},{2,3},{3,2},{4,5},{5,4},{6,7},{7,6},{8,9},{9,8},{10,11... | collective-permute-start | bytes 12296 | tf_op jit(solution)/shard_map/ppermute | solution.py:14
  40.7 13.4 %collective-permute-start.12 = (bf16[64,2048]{1,0:T(8,128)(2,1)S(1)}, bf16[64,2048]{1,0:T(8,128)(2,1)S(1)}, u32[]{:S(2)}, u32[]{:S(2)}) collective-permute-start(bf16[64,2048]{1,0:T(8,128)(2,1)S(1)} %get-tuple-element.23), channel_id=1, source_target_pairs={{0,48},{16,32},{32,16},{48,0},{64,112},{80,96},{96,80},{112,64},{1... | collective-permute-start | bytes 786440 | tf_op jit(solution)/shard_map/ppermute | solution.py:14
  41.8 20.0 %collective-permute-start.17 = (f32[16,1024]{1,0:T(8,128)S(1)}, f32[16,1024]{1,0:T(8,128)S(1)}, u32[]{:S(2)}, u32[]{:S(2)}) collective-permute-start(f32[16,1024]{1,0:T(8,128)S(1)} %get-tuple-element.52), channel_id=1, source_target_pairs={{0,1},{1,0},{2,3},{3,2},{4,5},{5,4},{6,7},{7,6},{8,9},{9,8},{10,11... | collective-permute-start | bytes 196616 | tf_op jit(solution)/shard_map/ppermute | solution.py:14
  115.7 14.9 %collective-permute-start.32 = (bf16[64,2048]{1,0:T(8,128)(2,1)S(1)}, bf16[64,2048]{1,0:T(8,128)(2,1)S(1)}, u32[]{:S(2)}, u32[]{:S(2)}) collective-permute-start(bf16[64,2048]{1,0:T(8,128)(2,1)S(1)} %pad_maximum_fusion.2.a0.refs_8_), channel_id=1, source_target_pairs={{0,6},{1,7},{2,4},{3,5},{4,2},{5,3},{6,0},{7,1},{8,14},{9,15},{10,... | collective-permute-start | bytes 786440 | tf_op jit(solution)/shard_map/ppermute | solution.py:14
  116.5 15.0 %collective-permute-start.31 = (bf16[64,2048]{1,0:T(8,128)(2,1)S(1)}, bf16[64,2048]{1,0:T(8,128)(2,1)S(1)}, u32[]{:S(2)}, u32[]{:S(2)}) collective-permute-start(bf16[64,2048]{1,0:T(8,128)(2,1)S(1)} %pad_maximum_fusion.2.a0.refs_8_), channel_id=1, source_target_pairs={{0,4},{1,5},{2,6},{3,7},{4,0},{5,1},{6,2},{7,3},{8,12},{9,13},{10,... | collective-permute-start | bytes 786440 | tf_op jit(solution)/shard_map/ppermute | solution.py:14
  116.5 15.0 %collective-permute-start.30 = (bf16[64,2048]{1,0:T(8,128)(2,1)S(1)}, bf16[64,2048]{1,0:T(8,128)(2,1)S(1)}, u32[]{:S(2)}, u32[]{:S(2)}) collective-permute-start(bf16[64,2048]{1,0:T(8,128)(2,1)S(1)} %pad_maximum_fusion.2.a0.refs_8_), channel_id=1, source_target_pairs={{0,2},{1,3},{2,0},{3,1},{4,6},{5,7},{6,4},{7,5},{8,10},{9,11},{10,... | collective-permute-start | bytes 786440 | tf_op jit(solution)/shard_map/ppermute | solution.py:14
  129.4 58.3 %collective-permute-start.5 = (bf16[64,2048]{1,0:T(8,128)(2,1)S(1)}, bf16[64,2048]{1,0:T(8,128)(2,1)S(1)}, u32[]{:S(2)}, u32[]{:S(2)}) collective-permute-start(bf16[64,2048]{1,0:T(8,128)(2,1)S(1)} %pad_maximum_fusion.a0.refs_0_), channel_id=1, source_target_pairs={{0,1},{1,0},{2,3},{3,2},{4,5},{5,4},{6,7},{7,6},{8,9},{9,8},{10,11... | collective-permute-start | bytes 786440 | tf_op jit(solution)/shard_map/ppermute | solution.py:14
  139.6 22.4 %collective-permute-start.45 = (bf16[64,2048]{1,0:T(8,128)(2,1)S(1)}, bf16[64,2048]{1,0:T(8,128)(2,1)S(1)}, u32[]{:S(2)}, u32[]{:S(2)}) collective-permute-start(bf16[64,2048]{1,0:T(8,128)(2,1)S(1)} %get-tuple-element.30), channel_id=1, source_target_pairs={{0,32},{16,48},{32,0},{48,16},{64,96},{80,112},{96,64},{112,80},{1... | collective-permute-start | bytes 786440 | tf_op jit(solution)/shard_map/ppermute | solution.py:14
  141.0 21.0 %collective-permute-start.46 = (bf16[64,2048]{1,0:T(8,128)(2,1)S(1)}, bf16[64,2048]{1,0:T(8,128)(2,1)S(1)}, u32[]{:S(2)}, u32[]{:S(2)}) collective-permute-start(bf16[64,2048]{1,0:T(8,128)(2,1)S(1)} %get-tuple-element.31), channel_id=1, source_target_pairs={{0,48},{16,32},{32,16},{48,0},{64,112},{80,96},{96,80},{112,64},{1... | collective-permute-start | bytes 786440 | tf_op jit(solution)/shard_map/ppermute | solution.py:14
  143.5 44.4 %collective-permute-start.8 = (bf16[64,2048]{1,0:T(8,128)(2,1)S(1)}, bf16[64,2048]{1,0:T(8,128)(2,1)S(1)}, u32[]{:S(2)}, u32[]{:S(2)}) collective-permute-start(bf16[64,2048]{1,0:T(8,128)(2,1)S(1)} %collective-permute-done.4.a3.refs_3_), channel_id=1, source_target_pairs={{0,1},{1,0},{2,3},{3,2},{4,5},{5,4},{6,7},{7,6},{8,9},{9,8},{10,11... | collective-permute-start | bytes 786440 | tf_op jit(solution)/shard_map/ppermute | solution.py:14
  149.6 16.7 %collective-permute-start.39 = (bf16[32,1024]{1,0:T(8,128)(2,1)S(1)}, bf16[32,1024]{1,0:T(8,128)(2,1)S(1)}, u32[]{:S(2)}, u32[]{:S(2)}) collective-permute-start(bf16[32,1024]{1,0:T(8,128)(2,1)S(1)} %pad_maximum_fusion.5), channel_id=1, source_target_pairs={{0,128},{16,144},{32,160},{48,176},{64,192},{80,208},{96,224},{112... | collective-permute-start | bytes 196616 | tf_op jit(solution)/shard_map/ppermute | solution.py:14
  170.7 20.0 %collective-permute-start.7 = (bf16[64,2048]{1,0:T(8,128)(2,1)S(1)}, bf16[64,2048]{1,0:T(8,128)(2,1)S(1)}, u32[]{:S(2)}, u32[]{:S(2)}) collective-permute-start(bf16[64,2048]{1,0:T(8,128)(2,1)S(1)} %collective-permute-done.3.a2.refs_2_), channel_id=1, source_target_pairs={{0,1},{1,0},{2,3},{3,2},{4,5},{5,4},{6,7},{7,6},{8,9},{9,8},{10,11... | collective-permute-start | bytes 786440 | tf_op jit(solution)/shard_map/ppermute | solution.py:14
  173.1 17.9 %collective-permute-start.6 = (bf16[64,2048]{1,0:T(8,128)(2,1)S(1)}, bf16[64,2048]{1,0:T(8,128)(2,1)S(1)}, u32[]{:S(2)}, u32[]{:S(2)}) collective-permute-start(bf16[64,2048]{1,0:T(8,128)(2,1)S(1)} %collective-permute-done.2.a1.refs_1_), channel_id=1, source_target_pairs={{0,1},{1,0},{2,3},{3,2},{4,5},{5,4},{6,7},{7,6},{8,9},{9,8},{10,11... | collective-permute-start | bytes 786440 | tf_op jit(solution)/shard_map/ppermute | solution.py:14
  186.9 14.4 %collective-permute-start.43 = (bf16[128,1024]{1,0:T(8,128)(2,1)S(1)}, bf16[128,1024]{1,0:T(8,128)(2,1)S(1)}, u32[]{:S(2)}, u32[]{:S(2)}) collective-permute-start(bf16[128,1024]{1,0:T(8,128)(2,1)S(1)} %constant_dynamic-update-slice_fusion.refs_16_), channel_id=1, source_target_pairs={{0,48},{16,32},{32,16},{48,0},{64,112},{80,96},{96,80},{112,64},{1... | collective-permute-start | bytes 786440 | tf_op jit(solution)/shard_map/ppermute | solution.py:14
  187.8 14.7 %collective-permute-start.51 = (bf16[32,1024]{1,0:T(8,128)(2,1)S(1)}, bf16[32,1024]{1,0:T(8,128)(2,1)S(1)}, u32[]{:S(2)}, u32[]{:S(2)}) collective-permute-start(bf16[32,1024]{1,0:T(8,128)(2,1)S(1)} %pad_maximum_fusion.6), channel_id=1, source_target_pairs={{0,64},{16,80},{32,96},{48,112},{64,0},{80,16},{96,32},{112,48},{1... | collective-permute-start | bytes 196616 | tf_op jit(solution)/shard_map/ppermute | solution.py:14
  187.9 30.2 %collective-permute-start.42 = (bf16[128,1024]{1,0:T(8,128)(2,1)S(1)}, bf16[128,1024]{1,0:T(8,128)(2,1)S(1)}, u32[]{:S(2)}, u32[]{:S(2)}) collective-permute-start(bf16[128,1024]{1,0:T(8,128)(2,1)S(1)} %constant_dynamic-update-slice_fusion.refs_16_), channel_id=1, source_target_pairs={{0,32},{16,48},{32,0},{48,16},{64,96},{80,112},{96,64},{112,80},{1... | collective-permute-start | bytes 786440 | tf_op jit(solution)/shard_map/ppermute | solution.py:14
  190.7 27.4 %collective-permute-start.41 = (bf16[128,1024]{1,0:T(8,128)(2,1)S(1)}, bf16[128,1024]{1,0:T(8,128)(2,1)S(1)}, u32[]{:S(2)}, u32[]{:S(2)}) collective-permute-start(bf16[128,1024]{1,0:T(8,128)(2,1)S(1)} %constant_dynamic-update-slice_fusion.refs_16_), channel_id=1, source_target_pairs={{0,16},{16,0},{32,48},{48,32},{64,80},{80,64},{96,112},{112,96},{1... | collective-permute-start | bytes 786440 | tf_op jit(solution)/shard_map/ppermute | solution.py:14
  191.0 28.0 %collective-permute-start.33 = (bf16[64,2048]{1,0:T(8,128)(2,1)S(1)}, bf16[64,2048]{1,0:T(8,128)(2,1)S(1)}, u32[]{:S(2)}, u32[]{:S(2)}) collective-permute-start(bf16[64,2048]{1,0:T(8,128)(2,1)S(1)} %pad_maximum_fusion.2.a0.refs_8_), channel_id=1, source_target_pairs={{0,1},{1,0},{2,3},{3,2},{4,5},{5,4},{6,7},{7,6},{8,9},{9,8},{10,11... | collective-permute-start | bytes 786440 | tf_op jit(solution)/shard_map/ppermute | solution.py:14
  201.2 17.7 %collective-permute-start.36 = (bf16[64,2048]{1,0:T(8,128)(2,1)S(1)}, bf16[64,2048]{1,0:T(8,128)(2,1)S(1)}, u32[]{:S(2)}, u32[]{:S(2)}) collective-permute-start(bf16[64,2048]{1,0:T(8,128)(2,1)S(1)} %collective-permute-done.32.a3.refs_11_), channel_id=1, source_target_pairs={{0,1},{1,0},{2,3},{3,2},{4,5},{5,4},{6,7},{7,6},{8,9},{9,8},{10,11... | collective-permute-start | bytes 786440 | tf_op jit(solution)/shard_map/ppermute | solution.py:14
  218.9 14.8 %collective-permute-start.56 = (bf16[128,1024]{1,0:T(8,128)(2,1)S(1)}, bf16[128,1024]{1,0:T(8,128)(2,1)S(1)}, u32[]{:S(2)}, u32[]{:S(2)}) collective-permute-start(bf16[128,1024]{1,0:T(8,128)(2,1)S(1)} %constant_dynamic-update-slice_fusion.5.refs_20_), channel_id=1, source_target_pairs={{0,48},{16,32},{32,16},{48,0},{64,112},{80,96},{96,80},{112,64},{1... | collective-permute-start | bytes 786440 | tf_op jit(solution)/shard_map/ppermute | solution.py:14
  219.0 14.8 %collective-permute-start.55 = (bf16[128,1024]{1,0:T(8,128)(2,1)S(1)}, bf16[128,1024]{1,0:T(8,128)(2,1)S(1)}, u32[]{:S(2)}, u32[]{:S(2)}) collective-permute-start(bf16[128,1024]{1,0:T(8,128)(2,1)S(1)} %constant_dynamic-update-slice_fusion.5.refs_20_), channel_id=1, source_target_pairs={{0,32},{16,48},{32,0},{48,16},{64,96},{80,112},{96,64},{112,80},{1... | collective-permute-start | bytes 786440 | tf_op jit(solution)/shard_map/ppermute | solution.py:14
  219.0 14.8 %collective-permute-start.54 = (bf16[128,1024]{1,0:T(8,128)(2,1)S(1)}, bf16[128,1024]{1,0:T(8,128)(2,1)S(1)}, u32[]{:S(2)}, u32[]{:S(2)}) collective-permute-start(bf16[128,1024]{1,0:T(8,128)(2,1)S(1)} %constant_dynamic-update-slice_fusion.5.refs_20_), channel_id=1, source_target_pairs={{0,16},{16,0},{32,48},{48,32},{64,80},{80,64},{96,112},{112,96},{1... | collective-permute-start | bytes 786440 | tf_op jit(solution)/shard_map/ppermute | solution.py:14
  (42 other events, 435.9 us)
